TPU v7x, 32 devices: a whole 2x2x4 slice. The times are simulated.
32 devices in a mesh: groups: 2 (over y), cells: 8 (over z, x), freq: 2 (over core).
Axes of the slice: x: 2, y: 2, z: 4, core: 2. Of those that a mesh axis runs over, the one named last changes fastest.
Arguments:
- adjoint: float32 [2, 256], P(None, ('groups', 'cells')), parts along dimension 1, may hold values from -6 to 6
- target_x: float32 [256], P(('groups', 'cells')), parts along dimension 0, may hold values from 0 to 1024
- target_y: float32 [256], P(('groups', 'cells')), parts along dimension 0, may hold values from 0 to 8
- target_z: float32 [256], P(('groups', 'cells')), parts along dimension 0, may hold values from 256 to 512
- assignment: int32 [256], P(('groups', 'cells')), parts along dimension 0, may hold values from 0 to 63
- level_codes: int32 [16384], P(('groups', 'cells', 'freq')), parts along dimension 0, may hold values from 0 to 15
- cell_params: bfloat16 [8, 16384], P(None, ('groups', 'cells', 'freq')), parts along dimension 1, may hold values from -5 to 5
- level_table: bfloat16 [16, 256], replicated, may hold values from -4 to 4
- w_proj: bfloat16 [8, 256], replicated, may hold values from -2 to 2
- w_one: bfloat16 [256, 256], replicated, may hold values from -0.375 to 0.375
- b_one: float32 [256], replicated, may hold values from -3 to 3
- w_two: bfloat16 [256, 256], replicated, may hold values from -0.375 to 0.375
- b_two: float32 [256], replicated, may hold values from -3 to 3
- w_out: bfloat16 [256, 128], replicated, may hold values from -0.375 to 0.375
Outputs:
- grad_out: float32 [512, 128], P('groups'), parts along dimension 0
- grad_w2: float32 [512, 256], P('groups'), parts along dimension 0
- grad_b2: float32 [512], P('groups'), parts along dimension 0
- grad_w1: float32 [512, 256], P('groups'), parts along dimension 0
- grad_b1: float32 [512], P('groups'), parts along dimension 0
- grad_table: float32 [32, 256], P('groups'), parts along dimension 0
- grad_proj: float32 [16, 256], P('groups'), parts along dimension 0
- grad_params: float32 [8, 16384], P(None, ('groups', 'cells', 'freq')), parts along dimension 1
There are 2 independent parts, one for each index of `groups`. A program takes and returns all parts, laid end to end along the dimension named above; an argument that names none is the same for every part. Nothing has to cross between parts.
All inputs are finite; a program needn't handle non-finite values.
Results may differ from a plain program's by a relative error of at most 0.01.
Values may be sent and summed in bfloat16 or wider, within the bound.
A program may use at most 64 MiB of HBM per device.

v0:
```python
import math
import jax
import jax.numpy as jnp
from jax import lax
from jax.sharding import PartitionSpec as P

SIDE = 1024
wave_low = 1.0
wave_high = 3.0
kernel_gain = 150.0


def silu_slope(value):
    sigma = jax.nn.sigmoid(value)
    return sigma * (1.0 + value * (1.0 - sigma))


def contract(left, right, left_dim, right_dim):
    return lax.dot_general(
        left, right, (((left_dim,), (right_dim,)), ((), ())), preferred_element_type=jnp.float32
    )


def kernel_tile(point_x, point_y, point_z, freq_value, cell_col, cell_row, count_freq):
    wave = wave_low + (wave_high - wave_low) * freq_value / (count_freq - 1)
    offset_x = point_x[:, None] - cell_col[None, :]
    offset_y = point_y[:, None] - cell_row[None, :]
    square = offset_x * offset_x + offset_y * offset_y + (point_z * point_z)[:, None]
    distance = jnp.sqrt(square)
    amplitude = kernel_gain * point_z[:, None] / square
    phase = wave[:, None] * distance
    return (
        (amplitude * jnp.cos(phase)).astype(jnp.bfloat16),
        (amplitude * jnp.sin(phase)).astype(jnp.bfloat16),
    )


def forward_pass(level_codes, cell_params, level_table, w_proj, w_one, b_one, w_two, b_two):
    levels = level_table.shape[0]
    onehot = (level_codes[:, None] == jnp.arange(levels, dtype=jnp.int32)[None, :]).astype(
        jnp.bfloat16
    )
    hidden_in = (
        jnp.dot(onehot, level_table, preferred_element_type=jnp.float32)
        + contract(cell_params, w_proj, 0, 0)
    ).astype(jnp.bfloat16)
    pre_one = jnp.dot(hidden_in, w_one, preferred_element_type=jnp.float32) + b_one
    act_one = jax.nn.silu(pre_one).astype(jnp.bfloat16)
    pre_two = jnp.dot(act_one, w_two, preferred_element_type=jnp.float32) + b_two
    act_two = jax.nn.silu(pre_two).astype(jnp.bfloat16)
    return (onehot, hidden_in, pre_one, act_one, pre_two, act_two)


def upper_grads(spectra, w_out, act_one, pre_two, act_two):
    back_two = contract(spectra, w_out, 0, 1)
    delta_two = (back_two * silu_slope(pre_two)).astype(jnp.bfloat16)
    grad_out = contract(act_two, spectra, 0, 1)
    grad_w2 = contract(act_one, delta_two, 0, 0)
    grad_b2 = jnp.sum(delta_two.astype(jnp.float32), axis=0)
    return ((grad_out, grad_w2, grad_b2), delta_two)


def lower_grads(delta_two, w_two, w_one, pre_one, hidden_in, onehot, cell_params, w_proj):
    back_one = contract(delta_two, w_two, 1, 1)
    delta_one = (back_one * silu_slope(pre_one)).astype(jnp.bfloat16)
    grad_w1 = contract(hidden_in, delta_one, 0, 0)
    grad_b1 = jnp.sum(delta_one.astype(jnp.float32), axis=0)
    back_zero = contract(delta_one, w_one, 1, 1).astype(jnp.bfloat16)
    grad_table = contract(onehot, back_zero, 0, 0)
    grad_proj = contract(cell_params, back_zero, 1, 0)
    grad_params = contract(w_proj, back_zero, 1, 1)
    return ((grad_w1, grad_b1, grad_table, grad_proj), grad_params)


def body(
    adjoint,
    target_x,
    target_y,
    target_z,
    assignment,
    level_codes,
    cell_params,
    level_table,
    w_proj,
    w_one,
    b_one,
    w_two,
    b_two,
    w_out,
):
    cell_count = level_codes.shape[0]
    freq_count = w_out.shape[1] // 2
    freq_size = lax.axis_size("freq")
    cell_rank = lax.axis_index("cells")
    freq_rank = lax.axis_index("freq")
    first_cell = (cell_rank * freq_size + freq_rank) * cell_count
    index = first_cell + jnp.arange(cell_count, dtype=jnp.int32)
    cell_col = (index % SIDE).astype(jnp.float32)
    cell_row = (index // SIDE).astype(jnp.float32)
    freq_grid = jnp.arange(freq_count, dtype=jnp.int32).astype(jnp.float32)
    stacked = jnp.concatenate(
        [
            adjoint,
            target_x[None, :],
            target_y[None, :],
            target_z[None, :],
            assignment.astype(jnp.float32)[None, :],
        ],
        axis=0,
    )
    initial = jnp.zeros((2 * freq_count, cell_count), jnp.float32)
    total = initial
    piece = lax.all_gather(stacked, "cells", axis=1, tiled=True)
    length = piece.shape[1]
    block_len = math.gcd(length, 256)
    sections = piece.reshape(6, length // block_len, block_len).transpose(1, 0, 2)

    def inner(accum, rows):
        adj_round = rows[0:2].astype(jnp.bfloat16)
        kre, kim = kernel_tile(rows[2], rows[3], rows[4], rows[5], cell_col, cell_row, freq_count)
        select = (rows[5][:, None] == freq_grid[None, :]).astype(jnp.bfloat16)
        part_a = select * adj_round[0][:, None]
        part_b = select * adj_round[1][:, None]
        left_re = jnp.concatenate([part_a, part_b], axis=1)
        left_im = jnp.concatenate([part_b, -part_a], axis=1)
        return (accum + contract(left_re, kre, 0, 0) + contract(left_im, kim, 0, 0), None)

    total, unused = lax.scan(inner, total, sections)
    local_spec = total.astype(jnp.bfloat16)
    scale = 1.0 / math.sqrt(cell_count * lax.axis_size("cells") * freq_size)
    onehot, hidden_in, pre_one, act_one, pre_two, act_two = forward_pass(
        level_codes, cell_params, level_table, w_proj, w_one, b_one, w_two, b_two
    )
    upper, delta_two = upper_grads(local_spec, w_out, act_one, pre_two, act_two)
    lower, grad_params = lower_grads(
        delta_two, w_two, w_one, pre_one, hidden_in, onehot, cell_params, w_proj
    )
    totals = lax.psum(
        (
            upper[0] * scale,
            upper[1] * scale,
            upper[2] * scale,
            lower[0] * scale,
            lower[1] * scale,
            lower[2] * scale,
            lower[3] * scale,
        ),
        ("cells", "freq"),
    )
    grad_out, grad_w2, grad_b2, grad_w1, grad_b1, grad_table, grad_proj = totals
    return (grad_out, grad_w2, grad_b2, grad_w1, grad_b1, grad_table, grad_proj, grad_params)


def solution(mesh):
    placed = (
        P(None, ("groups", "cells")),
        P(("groups", "cells")),
        P(("groups", "cells")),
        P(("groups", "cells")),
        P(("groups", "cells")),
        P(("groups", "cells", "freq")),
        P(None, ("groups", "cells", "freq")),
        P(),
        P(),
        P(),
        P(),
        P(),
        P(),
        P(),
    )
    return jax.shard_map(
        body,
        mesh=mesh,
        in_specs=placed,
        out_specs=(
            P("groups", None),
            P("groups", None),
            P("groups"),
            P("groups", None),
            P("groups"),
            P("groups", None),
            P("groups", None),
            P(None, ("groups", "cells", "freq")),
        ),
        check_vma=False,
    )
```

profile of v0, /device:TPU:0, one launch (start us, length us, event | category | flops | bytes accessed | tf_op | source)
XLA Modules:
  0.0 153.7 jit_solution(16663212163118805640)
XLA Ops:
  7.2 0.0 all-reduce.4.cloned.1.call-start
  7.3 0.7 copy-done.15
  7.9 0.6 copy-done.11
  8.6 0.0 copy-done.8
  8.7 32.4 %all-gather = f32[8,16,6]{1,2,0:T(8,128)S(1)} all-gather(f32[1,16,6]{1,2,0:T(8,128)S(1)} %bitcast.55), channel_id=1, replica_groups=mesh['groups'=2,'cells'=8,'freq'=2] {'cells'}, dimensions={0}, use_global_device_ids=true | all-gather | bytes 3456 | tf_op jit(solution)/shard_map/all_gather | solution.py:113
  41.1 0.1 reshape.88
  41.2 0.1 fusion.35
  41.4 1.2 fusion.7
  42.6 1.2 fusion.3
  43.9 0.3 fusion.6
  44.2 0.4 copy-done.4
  44.6 0.3 fusion
  44.9 0.6 copy-done.1
  45.5 0.2 convolution_add_fusion.2
  45.7 0.4 copy-done.14
  46.2 0.3 convolution_add_fusion.1
  46.4 1.0 convolution_multiply_fusion.4
  47.4 0.3 convert_reduce_fusion.1
  47.8 1.0 convolution_multiply_fusion.3
  48.8 0.3 convert_reduce_fusion
  49.1 1.0 convolution_multiply_fusion.2
  50.1 0.0 all-reduce.4.cloned.1.call-update
  50.2 0.3 convolution_convert_fusion
  50.4 0.1 fusion.4
  50.6 0.3 convolution_multiply_fusion.5
  50.9 57.9 %all-reduce = (f32[256]{0:T(256)}, f32[256]{0:T(256)}, f32[16,256]{1,0:T(8,128)}, f32[8,256]{1,0:T(8,128)}) all-reduce(f32[256]{0:T(256)S(1)} %broadcast_multiply_fusion.1, f32[256]{0:T(256)S(1)} %broadcast_multiply_fusion, ...), channel_id=1, replica_groups=mesh['groups'=2,'cells'=8,'freq'=2] {'cells','freq'}, use_global_device_ids=true, to_apply=%region_3.4 | all-reduce | flops 6656 | bytes 53248 | tf_op jit(solution)/shard_map/psum | solution.py:138
  108.7 0.8 convolution_bitcast_fusion
  109.5 34.0 %all-reduce.4.cloned.1.call-done = (f32[256,128]{1,0:T(8,128)}, f32[256,256]{1,0:T(8,128)}, f32[256,256]{1,0:T(8,128)}) async-done(((f32[256,128]{1,0:T(8,128)}, f32[256,256]{1,0:T(8,128)}, f32[256,256]{1,0:T(8,128)}), (f32[256,128]{1,0:T(8,128)}, f32[256,256]{1,0:T(8,128)}, f32[256,256]{1,0:T(8,128)})) %all-reduce.4.cloned.1.call-update) | async-done | bytes 655376 | tf_op jit(solution)/shard_map/psum | solution.py:138
  143.5 1.6 %copy.27 = f32[256,128]{1,0:T(8,128)} copy(f32[256,128]{1,0:T(8,128)} %get-tuple-element.49) | data formatting | bytes 262144
  145.1 0.7 copy.28
  145.8 0.3 copy-done.2
  146.2 0.7 copy.29
  (36 shorter events, 0.2 us)
Async XLA Ops:
  7.2 38.5 %copy-start = (bf16[256,256]{1,0:T(8,128)(2,1)S(1)}, bf16[256,256]{1,0:T(8,128)(2,1)}, u32[]{:S(2)}) copy-start(bf16[256,256]{1,0:T(8,128)(2,1)} %param.25) | copy-start | bytes 393220
  7.2 136.3 %all-reduce.4.cloned.1.call-start = ((), (), s32[]{:S(2)}) async-start(), calls=%async_computation | async-start | bytes 1310720 | tf_op jit(solution)/shard_map/psum | solution.py:138
  7.2 0.7 copy-start.15
  7.9 0.7 copy-start.11
  7.9 0.7 copy-start.12
  7.9 0.7 copy-start.8
  7.9 0.7 copy-start.10
  42.6 1.3 copy-start.6
  42.6 1.3 copy-start.7
  43.9 0.7 copy-start.4
  43.9 0.7 copy-start.5
  44.6 0.9 copy-start.1
  44.6 0.9 copy-start.9
  45.5 0.7 copy-start.14
  46.4 1.0 copy-start.13
  143.5 1.6 %copy-start.3 = (f32[256,256]{1,0:T(8,128)S(1)}, f32[256,256]{1,0:T(8,128)}, u32[]{:S(2)}) copy-start(f32[256,256]{1,0:T(8,128)} %get-tuple-element.50) | copy-start | bytes 786436
  145.1 1.0 copy-start.2
Sparse Core Ops, SparseCore 0:
  50.3 93.1 all-reduce.3
where the time goes:
time: 154 us
  blocking collectives  90.3 us (59%)
  waiting for transfers between devices  34 us (22%)
  between operations  14.2 us (9%)
  matrix products  8.64 us (6%)
  local copies, waits for them, and re-layouts  6.34 us (4%)
    psum x1, blocking collectives, body(): lax.psum((upper[0] * scale, upper[1] * scale, upper[2] * scale, lower[0]...  57.9 us
    psum x1, waiting for transfers between devices, body(): lax.psum((upper[0] * scale, upper[1] * scale, upper[2] * scale, lower[0]...  34 us
    all_gather x1, blocking collectives, body(): piece = lax.all_gather(stacked, 'cells', axis=1, tiled=True)  32.4 us
    dot_general x12, matrix products, contract(): lax.dot_general(left, right, (((left_dim,), (right_dim,)), ((), ())), pre...  7.85 us
    unnamed x36, local copies, waits for them, and re-layouts  6.31 us
  transfers between devices with their start and end apart: 1, of which 1 were waited for; matrix products, arithmetic and copies ran while one was open for 1% of the time, Pallas kernels for 0%

commit v1 on v0

--- a/solution.py
+++ b/solution.py
@@ -110,7 +110,16 @@
     )
     initial = jnp.zeros((2 * freq_count, cell_count), jnp.float32)
     total = initial
-    piece = lax.all_gather(stacked, "cells", axis=1, tiled=True)
+    ways = lax.axis_size("cells")
+    up = [(d, (d + 1) % ways) for d in range(ways)]
+    down = [(d, (d - 1) % ways) for d in range(ways)]
+    earlier, later = ([stacked], [stacked])
+    for _ in range(ways // 2):
+        earlier.append(lax.ppermute(earlier[-1], "cells", up))
+    for _ in range((ways - 1) // 2):
+        later.append(lax.ppermute(later[-1], "cells", down))
+    line = jnp.concatenate([*earlier[::-1], *later[1:]], axis=1)
+    piece = jnp.roll(line, (lax.axis_index("cells") - ways // 2) * stacked.shape[1], axis=1)
     length = piece.shape[1]
     block_len = math.gcd(length, 256)
     sections = piece.reshape(6, length // block_len, block_len).transpose(1, 0, 2)

time: 154 us -> 147 us (0.955)
  blocking collectives: 90.3 us -> 57.9 us
  starting transfers between devices: 0.04 us -> 15.5 us
  waiting for transfers between devices: 34 us -> 43.5 us
    all_gather x1 -> x0, blocking collectives: 32.4 us -> none  [body(): piece = lax.all_gather(stacked, 'cells', axis=1, tiled=True)]
    ppermute x0 -> x7, starting transfers between devices: none -> 15.5 us  [the longest x3 15.5 us: body(): later.append(lax.ppermute(later[-1], 'cells', down))]
    ppermute x0 -> x7, waiting for transfers between devices: none -> 12.5 us  [the longest x4 12.5 us: body(): earlier.append(lax.ppermute(earlier[-1], 'cells', up))]
    psum x1, waiting for transfers between devices: 34 us -> 31 us  [body(): lax.psum((upper[0] * scale, upper[1] * scale, upper[2] * scale, lower[0]...]
    unnamed x36 -> x33, local copies, waits for them, and re-layouts: 6.31 us -> 6.25 us
  transfers between devices with their start and end apart: 1 -> 8, of which waited for: 1 -> 5; matrix products, arithmetic and copies ran while one was open for 1% -> 1% of each run, Pallas kernels for 0% -> 0%
where the time goes in v1:
time: 147 us
  blocking collectives  57.9 us (39%)
  waiting for transfers between devices  43.5 us (30%)
  starting transfers between devices  15.5 us (11%)
  between operations  14.2 us (10%)
  matrix products  8.65 us (6%)
  local copies, waits for them, and re-layouts  6.36 us (4%)
    psum x1, blocking collectives, body(): lax.psum((upper[0] * scale, upper[1] * scale, upper[2] * scale, lower[0]...  57.9 us
    psum x1, waiting for transfers between devices, body(): lax.psum((upper[0] * scale, upper[1] * scale, upper[2] * scale, lower[0]...  31 us
    ppermute x3, starting transfers between devices, body(): later.append(lax.ppermute(later[-1], 'cells', down))  15.5 us
    ppermute x4, waiting for transfers between devices, body(): earlier.append(lax.ppermute(earlier[-1], 'cells', up))  12.5 us
    dot_general x12, matrix products, contract(): lax.dot_general(left, right, (((left_dim,), (right_dim,)), ((), ())), pre...  7.87 us
    unnamed x33, local copies, waits for them, and re-layouts  6.25 us
  transfers between devices with their start and end apart: 8, of which 5 were waited for; matrix products, arithmetic and copies ran while one was open for 1% of the time, Pallas kernels for 0%

profile of v1, /device:TPU:0, one launch (start us, length us, event | category | flops | bytes accessed | tf_op | source)
XLA Modules:
  0.0 147.0 jit_solution(11615873938099606438)
XLA Ops:
  7.2 0.7 convert_bitcast_fusion
  7.9 0.6 copy-done.11
  8.7 6.1 %collective-permute-start.4 = (f32[6,16]{1,0:T(8,128)S(1)}, f32[6,16]{1,0:T(8,128)S(1)}, u32[]{:S(2)}, u32[]{:S(2)}) collective-permute-start(f32[6,16]{1,0:T(8,128)S(1)} %concatenate.17), channel_id=1, source_target_pairs={{0,14},{2,0},{4,2},{6,4},{8,6},{10,8},{12,10},{14,12},{1,15},{3,1}... | collective-permute-start | bytes 1160 | tf_op jit(solution)/shard_map/ppermute | solution.py:120
  14.7 0.7 copy-done.6
  15.4 0.3 fusion.6
  15.7 0.4 copy-done.4
  16.1 0.3 fusion
  16.4 0.6 copy-done.1
  17.3 0.4 copy-done.14
  17.7 0.3 convolution_add_fusion.1
  18.0 3.0 %collective-permute-done = f32[6,16]{1,0:T(8,128)S(1)} collective-permute-done((f32[6,16]{1,0:T(8,128)S(1)}, f32[6,16]{1,0:T(8,128)S(1)}, u32[]{:S(2)}, u32[]{:S(2)}) %collective-permute-start) | collective-permute-done | bytes 416 | tf_op jit(solution)/shard_map/ppermute | solution.py:118
  21.0 4.7 %collective-permute-start.5 = (f32[6,16]{1,0:T(8,128)S(1)}, f32[6,16]{1,0:T(8,128)S(1)}, u32[]{:S(2)}, u32[]{:S(2)}) collective-permute-start(f32[6,16]{1,0:T(8,128)S(1)} %collective-permute-done.4), channel_id=1, source_target_pairs={{0,14},{2,0},{4,2},{6,4},{8,6},{10,8},{12,10},{14,12},{1,15},{3,1}... | collective-permute-start | bytes 1160 | tf_op jit(solution)/shard_map/ppermute | solution.py:120
  25.7 1.6 %collective-permute-done.1 = f32[6,16]{1,0:T(8,128)S(1)} collective-permute-done((f32[6,16]{1,0:T(8,128)S(1)}, f32[6,16]{1,0:T(8,128)S(1)}, u32[]{:S(2)}, u32[]{:S(2)}) %collective-permute-start.1) | collective-permute-done | bytes 416 | tf_op jit(solution)/shard_map/ppermute | solution.py:118
  27.3 4.7 %collective-permute-start.6 = (f32[6,16]{1,0:T(8,128)S(1)}, f32[6,16]{1,0:T(8,128)S(1)}, u32[]{:S(2)}, u32[]{:S(2)}) collective-permute-start(f32[6,16]{1,0:T(8,128)S(1)} %collective-permute-done.5), channel_id=1, source_target_pairs={{0,14},{2,0},{4,2},{6,4},{8,6},{10,8},{12,10},{14,12},{1,15},{3,1}... | collective-permute-start | bytes 1160 | tf_op jit(solution)/shard_map/ppermute | solution.py:120
  32.0 1.6 %collective-permute-done.2 = f32[6,16]{1,0:T(8,128)S(1)} collective-permute-done((f32[6,16]{1,0:T(8,128)S(1)}, f32[6,16]{1,0:T(8,128)S(1)}, u32[]{:S(2)}, u32[]{:S(2)}) %collective-permute-start.2) | collective-permute-done | bytes 416 | tf_op jit(solution)/shard_map/ppermute | solution.py:118
  33.6 6.3 %collective-permute-done.3 = f32[6,16]{1,0:T(8,128)S(1)} collective-permute-done((f32[6,16]{1,0:T(8,128)S(1)}, f32[6,16]{1,0:T(8,128)S(1)}, u32[]{:S(2)}, u32[]{:S(2)}) %collective-permute-start.3) | collective-permute-done | bytes 416 | tf_op jit(solution)/shard_map/ppermute | solution.py:118
  40.2 1.2 fusion.7
  41.5 1.2 fusion.3
  42.7 1.0 convolution_multiply_fusion.4
  43.7 0.3 convert_reduce_fusion.1
  44.0 1.0 convolution_multiply_fusion.3
  45.1 0.3 convert_reduce_fusion
  45.4 1.0 convolution_multiply_fusion.2
  46.4 0.3 convolution_convert_fusion
  46.8 0.3 convolution_multiply_fusion.5
  47.2 57.9 %all-reduce = (f32[256]{0:T(256)}, f32[256]{0:T(256)}, f32[16,256]{1,0:T(8,128)}, f32[8,256]{1,0:T(8,128)}) all-reduce(f32[256]{0:T(256)S(1)} %broadcast_multiply_fusion.1, f32[256]{0:T(256)S(1)} %broadcast_multiply_fusion, ...), channel_id=1, replica_groups=mesh['groups'=2,'cells'=8,'freq'=2] {'cells','freq'}, use_global_device_ids=true, to_apply=%region_3.4 | all-reduce | flops 6656 | bytes 53248 | tf_op jit(solution)/shard_map/psum | solution.py:147
  105.1 0.8 convolution_bitcast_fusion
  105.8 31.0 %all-reduce.4.cloned.1.call-done = (f32[256,128]{1,0:T(8,128)}, f32[256,256]{1,0:T(8,128)}, f32[256,256]{1,0:T(8,128)}) async-done(((f32[256,128]{1,0:T(8,128)}, f32[256,256]{1,0:T(8,128)}, f32[256,256]{1,0:T(8,128)}), (f32[256,128]{1,0:T(8,128)}, f32[256,256]{1,0:T(8,128)}, f32[256,256]{1,0:T(8,128)})) %all-reduce.4.cloned.1.call-update) | async-done | bytes 655376 | tf_op jit(solution)/shard_map/psum | solution.py:147
  136.8 1.6 %copy.25 = f32[256,128]{1,0:T(8,128)} copy(f32[256,128]{1,0:T(8,128)} %get-tuple-element.51) | data formatting | bytes 262144
  138.4 0.7 copy.26
  139.2 0.3 copy-done.2
  139.5 0.7 copy.27
  (46 shorter events, 0.9 us)
Async XLA Ops:
  7.2 10.1 %copy-start = (bf16[256,256]{1,0:T(8,128)(2,1)S(1)}, bf16[256,256]{1,0:T(8,128)(2,1)}, u32[]{:S(2)}) copy-start(bf16[256,256]{1,0:T(8,128)(2,1)} %param.25) | copy-start | bytes 393220
  7.2 129.6 %all-reduce.4.cloned.1.call-start = ((), (), s32[]{:S(2)}) async-start(), calls=%async_computation | async-start | bytes 1310720 | tf_op jit(solution)/shard_map/psum | solution.py:147
  7.9 0.7 copy-start.11
  7.9 0.7 copy-start.12
  7.9 0.7 copy-start.8
  7.9 0.7 copy-start.10
  8.7 12.4 %collective-permute-start.4 = (f32[6,16]{1,0:T(8,128)S(1)}, f32[6,16]{1,0:T(8,128)S(1)}, u32[]{:S(2)}, u32[]{:S(2)}) collective-permute-start(f32[6,16]{1,0:T(8,128)S(1)} %concatenate.17), channel_id=1, source_target_pairs={{0,14},{2,0},{4,2},{6,4},{8,6},{10,8},{12,10},{14,12},{1,15},{3,1}... | collective-permute-start | bytes 1160 | tf_op jit(solution)/shard_map/ppermute | solution.py:120
  14.7 6.3 %collective-permute-start = (f32[6,16]{1,0:T(8,128)S(1)}, f32[6,16]{1,0:T(8,128)S(1)}, u32[]{:S(2)}, u32[]{:S(2)}) collective-permute-start(f32[6,16]{1,0:T(8,128)S(1)} %concatenate.17), channel_id=1, source_target_pairs={{0,2},{2,4},{4,6},{6,8},{8,10},{10,12},{12,14},{14,0},{1,3},{3,5},... | collective-permute-start | bytes 1160 | tf_op jit(solution)/shard_map/ppermute | solution.py:118
  14.7 0.7 copy-start.6
  14.7 0.7 copy-start.7
  15.4 0.7 copy-start.4
  15.4 0.7 copy-start.5
  16.1 0.9 copy-start.1
  16.1 0.9 copy-start.9
  17.0 0.7 copy-start.14
  21.0 6.3 %collective-permute-start.1 = (f32[6,16]{1,0:T(8,128)S(1)}, f32[6,16]{1,0:T(8,128)S(1)}, u32[]{:S(2)}, u32[]{:S(2)}) collective-permute-start(f32[6,16]{1,0:T(8,128)S(1)} %collective-permute-done), channel_id=1, source_target_pairs={{0,2},{2,4},{4,6},{6,8},{8,10},{10,12},{12,14},{14,0},{1,3},{3,5},... | collective-permute-start | bytes 1160 | tf_op jit(solution)/shard_map/ppermute | solution.py:118
  21.0 6.3 %collective-permute-start.5 = (f32[6,16]{1,0:T(8,128)S(1)}, f32[6,16]{1,0:T(8,128)S(1)}, u32[]{:S(2)}, u32[]{:S(2)}) collective-permute-start(f32[6,16]{1,0:T(8,128)S(1)} %collective-permute-done.4), channel_id=1, source_target_pairs={{0,14},{2,0},{4,2},{6,4},{8,6},{10,8},{12,10},{14,12},{1,15},{3,1}... | collective-permute-start | bytes 1160 | tf_op jit(solution)/shard_map/ppermute | solution.py:120
  27.3 6.3 %collective-permute-start.2 = (f32[6,16]{1,0:T(8,128)S(1)}, f32[6,16]{1,0:T(8,128)S(1)}, u32[]{:S(2)}, u32[]{:S(2)}) collective-permute-start(f32[6,16]{1,0:T(8,128)S(1)} %collective-permute-done.1), channel_id=1, source_target_pairs={{0,2},{2,4},{4,6},{6,8},{8,10},{10,12},{12,14},{14,0},{1,3},{3,5},... | collective-permute-start | bytes 1160 | tf_op jit(solution)/shard_map/ppermute | solution.py:118
  27.3 6.3 %collective-permute-start.6 = (f32[6,16]{1,0:T(8,128)S(1)}, f32[6,16]{1,0:T(8,128)S(1)}, u32[]{:S(2)}, u32[]{:S(2)}) collective-permute-start(f32[6,16]{1,0:T(8,128)S(1)} %collective-permute-done.5), channel_id=1, source_target_pairs={{0,14},{2,0},{4,2},{6,4},{8,6},{10,8},{12,10},{14,12},{1,15},{3,1}... | collective-permute-start | bytes 1160 | tf_op jit(solution)/shard_map/ppermute | solution.py:120
  33.6 6.3 %collective-permute-start.3 = (f32[6,16]{1,0:T(8,128)S(1)}, f32[6,16]{1,0:T(8,128)S(1)}, u32[]{:S(2)}, u32[]{:S(2)}) collective-permute-start(f32[6,16]{1,0:T(8,128)S(1)} %collective-permute-done.2), channel_id=1, source_target_pairs={{0,2},{2,4},{4,6},{6,8},{8,10},{10,12},{12,14},{14,0},{1,3},{3,5},... | collective-permute-start | bytes 1160 | tf_op jit(solution)/shard_map/ppermute | solution.py:118
  42.7 1.0 copy-start.13
  136.8 1.6 %copy-start.3 = (f32[256,256]{1,0:T(8,128)S(1)}, f32[256,256]{1,0:T(8,128)}, u32[]{:S(2)}) copy-start(f32[256,256]{1,0:T(8,128)} %get-tuple-element.52) | copy-start | bytes 786436
  138.4 1.0 copy-start.2
Sparse Core Ops, SparseCore 0:
  47.3 89.5 all-reduce.3
